TPU v7x, 32 devices: a whole 2x2x4 slice. The times are simulated.
32 devices in a mesh: ctx: 8 (over y, x, core), chan: 4 (over z).
Axes of the slice: x: 2, y: 2, z: 4, core: 2. Of those that a mesh axis runs over, the one named last changes fastest.
Arguments:
- queries: bfloat16 [1024, 4096], P('ctx', 'chan'), may hold values from -8 to 8
- key_rows: bfloat16 [1024, 4096], P('ctx', 'chan'), may hold values from -8 to 8
- value_rows: bfloat16 [1024, 4096], P('ctx', 'chan'), may hold values from -16 to 16
- gate_in: bfloat16 [1024, 4096], P('ctx', 'chan'), may hold values from -6 to 6
- gate_out: bfloat16 [1024, 4096], P('ctx', 'chan'), may hold values from -6 to 6
- kernel_taps: float32 [512, 7], P('chan'), may hold values from -2 to 2
- norm_gain: float32 [4096], P('chan'), may hold values from 0.1 to 1.9
- cotangent: bfloat16 [1024, 4096], P('ctx', 'chan'), may hold values from -6 to 6
Outputs:
- mixed: bfloat16 [1024, 4096], P('ctx', 'chan')
- grad_queries: bfloat16 [1024, 4096], P('ctx', 'chan')
- grad_keys: bfloat16 [1024, 4096], P('ctx', 'chan')
- grad_values: bfloat16 [1024, 4096], P('ctx', 'chan')
- grad_gate_in: bfloat16 [1024, 4096], P('ctx', 'chan')
- grad_gate_out: bfloat16 [1024, 4096], P('ctx', 'chan')
- grad_filter: float32 [512, 7], P('chan')
- grad_gain: float32 [4096], P('chan')
All inputs are finite; a program needn't handle non-finite values.
Results may differ from a plain program's by a relative error of at most 0.015.
Values may be sent and summed in bfloat16 or wider, within the bound.
No kernel may reach another device: no remote copies, remote signals or barrier semaphores. Data moves between devices by JAX's collectives and lax.ppermute only.
A program may use at most 128 MiB of HBM per device.

v0:
```python
import jax
import jax.numpy as jnp
from jax import lax
from jax.sharding import PartitionSpec as P

HEAD = 128
FILT = 7
WIDTH = 4096
EPS = 1e-06
NEG = -1e30


def from_behind(shard, axis, by):
    length = lax.axis_size(axis)
    pairs = [(i, i + by) for i in range(length) if 0 <= i + by < length]
    return lax.ppermute(shard, axis, pairs)


def score_block(query_heads, key_block, query_pos, key_pos):
    scores = jnp.einsum(
        "rhe,khe->hrk", query_heads, key_block, preferred_element_type=jnp.float32
    ) * HEAD ** (-0.5)
    allowed = query_pos[:, None] >= key_pos[None, :]
    return jnp.where(allowed[None], scores, NEG)


def row_totals(query_heads, query_pos, block_count, keys_heads, block_rows):
    row_count = query_heads.shape[0]
    head_count = query_heads.shape[1]

    def advance(block_index, running):
        row_max, row_sum = running
        first_key = block_index * block_rows
        key_block = lax.dynamic_slice_in_dim(keys_heads, first_key, block_rows, 0)
        key_pos = first_key + jnp.arange(block_rows, dtype=jnp.int32)
        scores = score_block(query_heads, key_block, query_pos, key_pos)
        new_max = jnp.maximum(row_max, jnp.max(scores, axis=2))
        row_sum = row_sum * jnp.exp(row_max - new_max) + jnp.sum(
            jnp.exp(scores - new_max[:, :, None]), axis=2
        )
        return (new_max, row_sum)

    initial = (
        jnp.full((head_count, row_count), NEG, jnp.float32),
        jnp.zeros((head_count, row_count), jnp.float32),
    )
    row_max, row_sum = lax.fori_loop(0, block_count, advance, initial)
    return row_max + jnp.log(row_sum)


def row_outputs(query_heads, query_pos, block_count, keys_heads, values_heads, lse, block_rows):
    row_count = query_heads.shape[0]
    head_count = query_heads.shape[1]

    def advance(block_index, summed):
        first_key = block_index * block_rows
        key_block = lax.dynamic_slice_in_dim(keys_heads, first_key, block_rows, 0)
        value_block = lax.dynamic_slice_in_dim(values_heads, first_key, block_rows, 0)
        key_pos = first_key + jnp.arange(block_rows, dtype=jnp.int32)
        scores = score_block(query_heads, key_block, query_pos, key_pos)
        weights_low = jnp.exp(scores - lse[:, :, None]).astype(jnp.bfloat16)
        return summed + jnp.einsum(
            "hrk,khe->rhe", weights_low, value_block, preferred_element_type=jnp.float32
        )

    summed = lax.fori_loop(
        0, block_count, advance, jnp.zeros((row_count, head_count, HEAD), jnp.float32)
    )
    return summed.reshape(row_count, head_count * HEAD).astype(jnp.bfloat16)


def query_grads(
    query_heads, d_heads, query_pos, block_count, keys_heads, values_heads, lse, delta, block_rows
):
    row_count = query_heads.shape[0]
    head_count = query_heads.shape[1]

    def advance(block_index, summed):
        first_key = block_index * block_rows
        key_block = lax.dynamic_slice_in_dim(keys_heads, first_key, block_rows, 0)
        value_block = lax.dynamic_slice_in_dim(values_heads, first_key, block_rows, 0)
        key_pos = first_key + jnp.arange(block_rows, dtype=jnp.int32)
        scores = score_block(query_heads, key_block, query_pos, key_pos)
        weights = jnp.exp(scores - lse[:, :, None])
        d_probs = jnp.einsum(
            "rhe,khe->hrk", d_heads, value_block, preferred_element_type=jnp.float32
        )
        d_scores = (weights * (d_probs - delta[:, :, None])).astype(jnp.bfloat16)
        return summed + jnp.einsum(
            "hrk,khe->rhe", d_scores, key_block, preferred_element_type=jnp.float32
        )

    summed = lax.fori_loop(
        0, block_count, advance, jnp.zeros((row_count, head_count, HEAD), jnp.float32)
    )
    return (summed * HEAD ** (-0.5)).reshape(row_count, head_count * HEAD).astype(jnp.bfloat16)


def shards(queries, key_rows, value_rows, gate_in, gate_out, kernel_taps, norm_gain, cotangent):
    row_count = queries.shape[0]
    channels = queries.shape[1]
    head_count = channels // HEAD
    group_count = kernel_taps.shape[0]
    devices = lax.axis_size("ctx")
    position = lax.axis_index("ctx")
    own_first = position * row_count
    total_rows = row_count * devices
    block_rows = min(512, total_rows)
    local_pos = jnp.arange(row_count, dtype=jnp.int32)
    keys_all, values_all = (
        lax.all_gather(key_rows, "ctx", axis=0, tiled=True),
        lax.all_gather(value_rows, "ctx", axis=0, tiled=True),
    )
    keys_heads = keys_all.reshape(total_rows, head_count, HEAD)
    query_sets = (queries, own_first + local_pos)
    query_block, query_pos = query_sets
    block_count = query_pos[-1] // block_rows + 1
    lse_sets = row_totals(
        query_block.reshape(-1, head_count, HEAD), query_pos, block_count, keys_heads, block_rows
    )
    values_heads = values_all.reshape(total_rows, head_count, HEAD)
    query_block, query_pos = query_sets
    outputs = row_outputs(
        query_block.reshape(-1, head_count, HEAD),
        query_pos,
        block_count,
        keys_heads,
        values_heads,
        lse_sets,
        block_rows,
    )
    lse_rows = lse_sets.T
    attn_wide = outputs.astype(jnp.float32)
    square_sum = lax.psum(jnp.sum(attn_wide * attn_wide, axis=1), "chan")
    inverse_rms = 1.0 / jnp.sqrt(square_sum / WIDTH + EPS)
    normed = attn_wide * inverse_rms[:, None] * norm_gain[None, :]
    gate_wide = gate_in.astype(jnp.float32)
    mixed_in = gate_wide * normed
    taps = jnp.broadcast_to(
        kernel_taps[:, None, :], (group_count, channels // group_count, FILT)
    ).reshape(channels, FILT)
    rim_before = from_behind(mixed_in[row_count - (FILT - 1) :], "ctx", 1)
    extended = jnp.concatenate([rim_before, mixed_in], axis=0)
    conv_out = jnp.zeros((row_count, channels), jnp.float32)
    for lag in range(FILT):
        conv_out = (
            conv_out + taps[:, lag][None, :] * extended[FILT - 1 - lag : FILT - 1 - lag + row_count]
        )
    out_gate = gate_out.astype(jnp.float32)
    mixed = (out_gate * conv_out).astype(jnp.bfloat16)
    upstream = cotangent.astype(jnp.float32)
    grad_gate_out = (upstream * conv_out).astype(jnp.bfloat16)
    d_conv = upstream * out_gate
    tap_columns = []
    for lag in range(FILT):
        per_channel = jnp.sum(
            d_conv * extended[FILT - 1 - lag : FILT - 1 - lag + row_count], axis=0
        )
        tap_columns.append(per_channel.reshape(group_count, -1).sum(axis=1))
    tap_terms = jnp.stack(tap_columns, axis=1)
    rim_after = from_behind(d_conv[: FILT - 1], "ctx", -1)
    extended_grad = jnp.concatenate([d_conv, rim_after], axis=0)
    d_mixed = jnp.zeros((row_count, channels), jnp.float32)
    for lag in range(FILT):
        d_mixed = d_mixed + taps[:, lag][None, :] * extended_grad[lag : lag + row_count]
    grad_gate_in = (d_mixed * normed).astype(jnp.bfloat16)
    d_normed = d_mixed * gate_wide
    gain_terms = jnp.sum(d_normed * attn_wide * inverse_rms[:, None], axis=0)
    grad_filter, grad_gain = lax.psum((tap_terms, gain_terms), "ctx")
    scaled = d_normed * norm_gain[None, :]
    row_dot = lax.psum(jnp.sum(scaled * attn_wide, axis=1), "chan")
    d_attn = (
        inverse_rms[:, None] * scaled - attn_wide * (inverse_rms**3 * row_dot / WIDTH)[:, None]
    ).astype(jnp.bfloat16)
    d_heads = d_attn.reshape(row_count, head_count, HEAD)
    delta_rows = jnp.sum(
        d_heads.astype(jnp.float32) * attn_wide.reshape(row_count, head_count, HEAD), axis=2
    )
    own_count = (own_first + row_count - 1) // block_rows + 1
    grad_queries = query_grads(
        queries.reshape(row_count, head_count, HEAD),
        d_heads,
        own_first + local_pos,
        own_count,
        keys_heads,
        values_heads,
        lse_rows.T,
        delta_rows.T,
        block_rows,
    )
    lse_all, delta_all = (
        lax.all_gather(lse_rows, "ctx", axis=0, tiled=True),
        lax.all_gather(delta_rows, "ctx", axis=0, tiled=True),
    )
    own_keys = key_rows.reshape(row_count, head_count, HEAD)
    own_values = value_rows.reshape(row_count, head_count, HEAD)
    key_pos = own_first + local_pos
    empty_grad = jnp.zeros((row_count, head_count, HEAD), jnp.float32)
    query_piece = lax.all_gather(queries, "ctx", axis=0, tiled=True)
    d_piece = lax.all_gather(d_attn, "ctx", axis=0, tiled=True)
    piece_rows = query_piece.shape[0]

    def contribute(totals):
        query_heads = query_piece.reshape(piece_rows, head_count, HEAD)
        piece_heads = d_piece.reshape(piece_rows, head_count, HEAD)
        query_pos = jnp.arange(piece_rows, dtype=jnp.int32)
        lse_piece = lse_all.T
        delta_piece = delta_all.T
        scores = score_block(query_heads, own_keys, query_pos, key_pos)
        weights = jnp.exp(scores - lse_piece[:, :, None])
        d_probs = jnp.einsum(
            "rhe,khe->hrk", piece_heads, own_values, preferred_element_type=jnp.float32
        )
        d_scores = (weights * (d_probs - delta_piece[:, :, None])).astype(jnp.bfloat16)
        key_grad = jnp.einsum(
            "hrk,rhe->khe", d_scores, query_heads, preferred_element_type=jnp.float32
        )
        value_grad = jnp.einsum(
            "hrk,rhe->khe",
            weights.astype(jnp.bfloat16),
            piece_heads,
            preferred_element_type=jnp.float32,
        )
        return (key_grad, value_grad)

    def unchanged(totals):
        return totals

    key_grad, value_grad = lax.cond(
        jnp.int32(0) + piece_rows > own_first, contribute, unchanged, (empty_grad, empty_grad)
    )
    grad_keys = (key_grad * HEAD ** (-0.5)).reshape(row_count, channels).astype(jnp.bfloat16)
    grad_values = value_grad.reshape(row_count, channels).astype(jnp.bfloat16)
    return (
        mixed,
        grad_queries,
        grad_keys,
        grad_values,
        grad_gate_in,
        grad_gate_out,
        grad_filter,
        grad_gain,
    )


def solution(mesh):
    placed = (
        P("ctx", "chan"),
        P("ctx", "chan"),
        P("ctx", "chan"),
        P("ctx", "chan"),
        P("ctx", "chan"),
        P("chan", None),
        P("chan"),
        P("ctx", "chan"),
    )
    return jax.shard_map(
        shards,
        mesh=mesh,
        in_specs=placed,
        out_specs=(
            P("ctx", "chan"),
            P("ctx", "chan"),
            P("ctx", "chan"),
            P("ctx", "chan"),
            P("ctx", "chan"),
            P("ctx", "chan"),
            P("chan", None),
            P("chan"),
        ),
        check_vma=False,
    )
```

profile of v0, /device:TPU:0, one launch (start us, length us, event | category | flops | bytes accessed | tf_op | source)
XLA Modules:
  0.0 189.7 jit_solution(9424736942254590684)
XLA Ops:
  7.2 1.8 copy.75
  9.1 1.8 copy.74
  11.0 1.1 convert_multiply_fusion.1
  12.1 0.8 copy-done.3
  12.9 1.3 collective-permute-start.1
  14.3 0.6 slice.80
  16.8 0.2 copy.76
  17.7 0.2 copy.80
  17.9 0.2 broadcast_in_dim.76
  18.1 0.2 reshape.211
  18.3 23.0 %all-gather.7.cloned.1.call-done = bf16[1024,1024]{0,1:T(8,128)(2,1)} async-done(((bf16[128,1024]{0,1:T(8,128)(2,1)}), bf16[1024,1024]{0,1:T(8,128)(2,1)}) %all-gather.7.cloned.1.call-update) | async-done | bytes 2097168 | tf_op jit(solution)/shard_map/all_gather | solution.py:111
  41.3 3.0 %copy.79 = bf16[1024,8,128]{2,0,1:T(8,128)(2,1)S(1)} copy(bf16[1024,8,128]{0,2,1:T(8,128)(2,1)} %bitcast.151) | data formatting | bytes 4194304
  44.4 1.2 while.35
  44.4 0.1 broadcast_compare_fusion.6
  44.6 0.5 fusion.130
  45.1 0.4 exponential_reduce_fusion.2
  45.6 26.3 %all-gather.5.cloned.1.call-done = bf16[1024,1024]{0,1:T(8,128)(2,1)} async-done(((bf16[128,1024]{0,1:T(8,128)(2,1)}), bf16[1024,1024]{0,1:T(8,128)(2,1)}) %all-gather.5.cloned.1.call-update) | async-done | bytes 2097168 | tf_op jit(solution)/shard_map/all_gather | solution.py:112
  71.9 2.4 %while.36 = (s32[]{:T(128)}, f32[128,8,128]{0,2,1:T(8,128)S(1)}, s32[]{:T(128)}, bf16[1024,8,128]{0,2,1:T(8,128)(2,1)}, bf16[1024,8,128]{2,0,1:T(8,128)(2,1)S(1)...) while((s32[]{:T(128)}, f32[128,8,128]{0,2,1:T(8,128)S(1)}, ...), condition=%wide.region_5.6_spmd.clone, body=%wide.region_4.5_spmd.clone.sunk | while | flops 270729856 | bytes 3549363 | solution.py:66
  72.0 0.1 broadcast_compare_fusion.7
  72.1 2.2 %fusion.134 = f32[128,8,128]{0,2,1:T(8,128)S(1)} fusion(f32[128,8,128]{0,2,1:T(8,128)S(1)} %get-tuple-element.657, bf16[128,8,128]{2,0,1:T(8,128)(2,1)S(1)} %get-tuple-element.673, f32[8,128]{1,0:T(8,128)S(1)} %get-tuple-element.674, bf16[1024,8,128]{2,0,1:T(8,128)(2,1)S(1)} %get-tuple-element.672, s32[]{:T(128)S(6)} %select_n.93, ...), kind=kOutput, calls=%fused_computation.44.clone.1 | convolution fusion | flops 270663680 | bytes 3478528 | tf_op jit(solution)/shard_map/while/body/hrk,khe->rhe/dot_general | solution.py:62
  74.4 1.0 multiply_reduce_fusion.10
  75.3 11.7 %psum.28 = f32[128]{0:T(128)S(1)} all-reduce(f32[128]{0:T(128)S(1)} %get-tuple-element.441), channel_id=1, replica_groups=mesh['ctx'=8,'chan'=4] {'chan'}, use_global_device_ids=true, to_apply=%region_7.8 | all-reduce | flops 128 | bytes 1024 | tf_op jit(solution)/shard_map/psum | solution.py:134
  87.0 1.2 copy.97
  88.3 4.0 %multiply_convert_fusion.1 = (bf16[128,1024]{1,0:T(8,128)(2,1)}, f32[128,1024]{1,0:T(8,128)S(1)}) fusion(f32[128,1024]{1,0:T(8,128)S(1)} %copy.97, f32[1024]{0:T(1024)S(1)} %copy-done.10, f32[128]{0:T(128)S(1)} %add_rsqrt_fusion, f32[6,1024]{1,0:T(8,128)S(1)} %collective-permute-done.1, f32[128,1024]{1,0:T(8,128)} %copy-done.3, f32[1024]{0:T(1024)S(1)} %bitcast.162, ...), kind=kLoop, calls=%fused_computation.133 | loop fusion | flops 3014656 | bytes 1892864 | tf_op jit(solution)/shard_map/convert_element_type | solution.py:166
  92.3 0.8 copy-done.1
  93.1 0.2 multiply_reduce_fusion
  93.3 8.4 %psum.29 = f32[128]{0:T(128)S(1)} all-reduce(f32[128]{0:T(128)S(1)} %get-tuple-element.373), channel_id=1, replica_groups=mesh['ctx'=8,'chan'=4] {'chan'}, use_global_device_ids=true, to_apply=%region_9.10 | all-reduce | flops 128 | bytes 1024 | tf_op jit(solution)/shard_map/psum | solution.py:171
  101.7 2.0 %subtract_convert_fusion = (bf16[128,1024]{1,0:T(8,128)(2,1)}, f32[128,1024]{1,0:T(8,128)S(1)}) fusion(f32[128,1024]{1,0:T(8,128)S(1)} %copy.97, f32[128]{0:T(128)S(1)} %fusion.102, f32[1024]{0:T(1024)S(1)} %copy-done.10, f32[128]{0:T(128)S(1)} %add_rsqrt_fusion, f32[128,1024]{1,0:T(8,128)} %copy-done.1, bf16[128,1024]{1,0:T(8,128)(2,1)} %param.19), kind=kLoop, calls=%fused_computation.137 | loop fusion | flops 1310720 | bytes 2102272 | tf_op jit(solution)/shard_map/convert_element_type | solution.py:174
  103.8 0.6 slice.103
  104.4 1.3 collective-permute-start
  105.7 1.0 copy.109
  106.7 0.2 copy.82
  106.9 1.1 multiply_reduce_fusion.8
  108.0 1.0 copy_bitcast_fusion
  109.0 0.9 broadcast.128
  109.9 5.9 %while.37 = (s32[]{:T(128)}, f32[128,8,128]{0,2,1:T(8,128)}, s32[]{:T(128)}, bf16[1024,8,128]{2,0,1:T(8,128)(2,1)S(1)}, bf16[128,8,128]{2,0,1:T(8,128)(2,1)S(1)}...) while((s32[]{:T(128)}, f32[128,8,128]{0,2,1:T(8,128)}, ...), condition=%wide.region_12.13_spmd.clone, body=%wide.region_11.12_spmd.clone.sunk | while | flops 405996160 | bytes 9058503 | solution.py:93
  109.9 1.7 fusion.140
  111.7 0.1 broadcast_compare_fusion.8
  111.8 4.1 %fusion.141 = f32[128,8,128]{0,2,1:T(8,128)} fusion(f32[128,8,128]{0,2,1:T(8,128)} %get-tuple-element.695, f32[8,512,128]{2,1,0:T(8,128)} %fusion.140, bf16[128,8,128]{2,0,1:T(8,128)(2,1)S(1)} %get-tuple-element.715, f32[8,128]{1,0:T(8,128)S(1)} %get-tuple-element.716, bf16[1024,8,128]{0,2,1:T(8,128)(2,1)} %get-tuple-element.714, s32[]{:T(128)S(6)} %select_n.95, ...), kind=kOutput, calls=%fused_computation.64.clone.1 | convolution fusion | flops 271712256 | bytes 5579776 | tf_op jit(solution)/shard_map/while/body/hrk,khe->rhe/dot_general | solution.py:89
  115.9 1.1 multiply_convert_fusion.3
  117.0 0.9 copy.98
  117.9 17.9 %all_gather.23 = f32[1024,8]{0,1:T(8,128)S(1)} all-gather(f32[128,8]{0,1:T(8,128)S(1)} %bitcast.178), channel_id=1, replica_groups=mesh['ctx'=8,'chan'=4] {'ctx'}, dimensions={0}, use_global_device_ids=true | all-gather | bytes 36864 | tf_op jit(solution)/shard_map/all_gather | solution.py:193
  135.8 8.5 %all_gather.21 = f32[1024,8]{0,1:T(8,128)S(1)} all-gather(f32[128,8]{0,1:T(8,128)S(1)} %bitcast.179), channel_id=1, replica_groups=mesh['ctx'=8,'chan'=4] {'ctx'}, dimensions={0}, use_global_device_ids=true | all-gather | bytes 36864 | tf_op jit(solution)/shard_map/all_gather | solution.py:192
  144.3 1.2 fusion.78
  145.5 1.2 multiply_reduce_fusion.1
  146.9 0.1 reshape.217
  147.0 0.1 reshape.219
  147.4 0.1 reduce_sum.175
  147.5 0.1 reduce_sum.177
  147.6 0.1 reduce_sum.179
  147.7 0.1 reduce_sum.181
  147.8 0.1 reduce_sum.183
  148.0 0.1 reduce_sum.185
  148.1 0.1 reduce_sum.187
  148.2 14.2 %all-reduce = (f32[128,7]{0,1:T(8,128)}, f32[1024]{0:T(1024)}) all-reduce(f32[128,7]{0,1:T(8,128)S(1)} %stack.31, f32[1024]{0:T(1024)S(1)} %get-tuple-element.372), channel_id=1, replica_groups=mesh['ctx'=8,'chan'=4] {'ctx'}, use_global_device_ids=true, to_apply=%region_29.30 | all-reduce | flops 1920 | bytes 15360 | tf_op jit(solution)/shard_map/psum | solution.py:169
  162.5 19.8 %conditional.1 = (f32[128,8,128]{0,2,1:T(8,128)S(1)}, bf16[128,1024]{1,0:T(8,128)(2,1)}) conditional(s32[]{:T(128)} %convert_element_type.91, () %tuple.33, (s32[128]{0:T(128)S(1)}, bf16[1024,1024]{1,0:T(8,128)(2,1)}, bf16[128,1024]{1,0:T(8,128)(2,1)S(1)}, f32[1024,8]{0,1:T(8,128)S(1)}, bf16[1024,1024]{1,0:T(8,128)(2,1)}, ...), branch_computations={%region_13.14_spmd, %region_14.15_spmd} | conditional | flops 1084489728 | bytes 38503096 | solution.py:229
  162.5 4.3 %fusion.11 = f32[8,1024,128]{2,1,0:T(8,128)} fusion(bf16[1024,1024]{1,0:T(8,128)(2,1)} %get-tuple-element.149, bf16[128,1024]{1,0:T(8,128)(2,1)S(1)} %get-tuple-element.150), kind=kOutput, calls=%fused_computation.9 | convolution fusion | flops 268435456 | bytes 6553600 | tf_op jit(solution)/shard_map/cond/branch_1_fun/rhe,khe->hrk/dot_general | solution.py:20
  166.8 4.1 %copy.88 = bf16[1024,1024]{0,1:T(8,128)(2,1)} copy(bf16[1024,1024]{1,0:T(8,128)(2,1)} %get-tuple-element.359) | data formatting | bytes 4194304 | tf_op jit(solution)/shard_map
  170.9 0.1 iota_compare_fusion
  171.0 6.4 %fusion.19 = f32[128,8,128]{2,0,1:T(8,128)S(1)} fusion(f32[8,1024,128]{2,1,0:T(8,128)} %fusion.11, bf16[1024,8,128]{0,2,1:T(8,128)(2,1)} %bitcast.152, f32[8,1024]{1,0:T(8,128)S(1)} %bitcast.174, f32[8,1024]{1,0:T(8,128)S(1)} %bitcast.176, pred[1024,128]{1,0:T(8,128)(4,1)S(1)} %iota_compare_fusion, bf16[1024,1024]{1,0:T(8,128)(2,1)S(1)} %copy-done.4, ...), kind=kOutput, calls=%fused_computation.17 | convolution fusion | flops 543162368 | bytes 9371648 | tf_op jit(solution)/shard_map/cond/branch_1_fun/hrk,rhe->khe/dot_general | solution.py:215
  177.4 0.2 copy.101
  177.6 3.8 %fusion.22 = bf16[8,128,128]{1,2,0:T(8,128)(2,1)S(1)} fusion(bf16[1024,8,128]{0,2,1:T(8,128)(2,1)} %bitcast.153, f32[8,1024,128]{2,1,0:T(8,128)} %fusion.11, f32[8,1024]{1,0:T(8,128)} %bitcast.175, pred[1024,128]{1,0:T(8,128)(4,1)S(1)} %iota_compare_fusion), kind=kOutput, calls=%fused_computation.18 | convolution fusion | flops 272760832 | bytes 6717440 | tf_op jit(solution)/shard_map/cond/branch_1_fun/hrk,rhe->khe/dot_general | solution.py:218
  181.4 0.9 copy.103
  182.3 0.9 copy.99
  (67 shorter events, 0.9 us)
Async XLA Ops:
  7.2 9.7 %copy-start.6 = (bf16[128,1024]{1,0:T(8,128)(2,1)S(1)}, bf16[128,1024]{1,0:T(8,128)(2,1)}, u32[]{:S(2)}) copy-start(bf16[128,1024]{1,0:T(8,128)(2,1)} %param.16) | copy-start | bytes 786436
  7.2 10.7 %copy-start.15 = (f32[128,7]{0,1:T(8,128)S(1)}, f32[128,7]{0,1:T(8,128)}, u32[]{:S(2)}) copy-start(f32[128,7]{0,1:T(8,128)} %param.21) | copy-start | bytes 10756
  7.2 34.1 %all-gather.7.cloned.1.call-start = ((), (), s32[]{:S(2)}) async-start(), calls=%async_computation.1 | async-start | bytes 2359296 | tf_op jit(solution)/shard_map/all_gather | solution.py:111
  9.1 62.8 %all-gather.5.cloned.1.call-start = ((), (), s32[]{:S(2)}) async-start(), calls=%async_computation | async-start | bytes 2359296 | tf_op jit(solution)/shard_map/all_gather | solution.py:112
  10.9 151.5 %all-gather.9.cloned.1.call-start = ((), (), s32[]{:S(2)}) async-start(), calls=%async_computation.2 | async-start | bytes 2359296 | tf_op jit(solution)/shard_map/all_gather | solution.py:199
  12.1 0.8 copy-start.3
  12.9 75.4 %collective-permute-start.1 = (f32[6,1024]{1,0:T(8,128)S(1)}, f32[6,1024]{1,0:T(8,128)S(1)}, u32[]{:S(2)}, u32[]{:S(2)}) collective-permute-start(f32[6,1024]{1,0:T(8,128)S(1)} %slice.119), channel_id=1, source_target_pairs={{4,0},{8,4},{12,8},{16,12},{20,16},{24,20},{28,24},{5,1},{9,5},{13... | collective-permute-start | bytes 73736 | tf_op jit(solution)/shard_map/ppermute | solution.py:16
  14.2 148.2 %all-gather.11.cloned.1.call-start = ((), (), s32[]{:S(2)}) async-start(), calls=%async_computation.3 | async-start | bytes 2359296 | tf_op jit(solution)/shard_map/all_gather | solution.py:200
  74.3 19.0 %copy-start = (f32[128,8,128]{0,2,1:T(8,128)}, f32[128,8,128]{0,2,1:T(8,128)S(1)}, u32[]{:S(2)}) copy-start(f32[128,8,128]{0,2,1:T(8,128)S(1)} %get-tuple-element.171) | copy-start | bytes 1572868
  74.4 13.9 %copy-start.10 = (f32[1024]{0:T(1024)S(1)}, f32[1024]{0:T(1024)}, u32[]{:S(2)}) copy-start(f32[1024]{0:T(1024)} %param.22) | copy-start | bytes 12292
  88.3 4.9 %copy-start.7 = (bf16[128,1024]{1,0:T(8,128)(2,1)S(1)}, bf16[128,1024]{1,0:T(8,128)(2,1)}, u32[]{:S(2)}) copy-start(bf16[128,1024]{1,0:T(8,128)(2,1)} %param.19) | copy-start | bytes 786436
  92.3 0.8 copy-start.1
  104.4 39.9 %collective-permute-start = (f32[6,1024]{1,0:T(8,128)}, f32[6,1024]{1,0:T(8,128)S(1)}, u32[]{:S(2)}, u32[]{:S(2)}) collective-permute-start(f32[6,1024]{1,0:T(8,128)} %slice.103), channel_id=1, source_target_pairs={{0,4},{4,8},{8,12},{12,16},{16,20},{20,24},{24,28},{1,5},{5,9},{9,... | collective-permute-start | bytes 73736 | tf_op jit(solution)/shard_map/ppermute | solution.py:16
  109.9 34.4 %copy-start.2 = (bf16[128,1024]{1,0:T(8,128)(2,1)S(1)}, bf16[128,1024]{1,0:T(8,128)(2,1)}, u32[]{:S(2)}) copy-start(bf16[128,1024]{1,0:T(8,128)(2,1)} %param.23) | copy-start | bytes 786436
  115.9 29.6 %copy-start.8 = (bf16[128,1024]{1,0:T(8,128)(2,1)S(1)}, bf16[128,1024]{1,0:T(8,128)(2,1)}, u32[]{:S(2)}) copy-start(bf16[128,1024]{1,0:T(8,128)(2,1)} %param.20) | copy-start | bytes 786436
  144.3 18.1 %copy-start.5 = (bf16[128,1024]{1,0:T(8,128)(2,1)S(1)}, bf16[128,1024]{1,0:T(8,128)(2,1)}, u32[]{:S(2)}) copy-start(bf16[128,1024]{1,0:T(8,128)(2,1)} %param.17) | copy-start | bytes 786436
  162.5 4.3 %copy-start.11 = (f32[1024,8]{0,1:T(8,128)}, f32[1024,8]{0,1:T(8,128)S(1)}, u32[]{:S(2)}) copy-start(f32[1024,8]{0,1:T(8,128)S(1)} %get-tuple-element.154) | copy-start | bytes 98308 | tf_op jit(solution)/shard_map/cond
  162.5 4.3 %copy-start.13 = (f32[1024,8]{0,1:T(8,128)}, f32[1024,8]{0,1:T(8,128)S(1)}, u32[]{:S(2)}) copy-start(f32[1024,8]{0,1:T(8,128)S(1)} %get-tuple-element.151) | copy-start | bytes 98308 | tf_op jit(solution)/shard_map/cond
  166.7 4.2 %copy-start.4 = (bf16[1024,1024]{1,0:T(8,128)(2,1)S(1)}, bf16[1024,1024]{1,0:T(8,128)(2,1)}, u32[]{:S(2)}) copy-start(bf16[1024,1024]{1,0:T(8,128)(2,1)} %get-tuple-element.149) | copy-start | bytes 6291460 | tf_op jit(solution)/shard_map/cond
  166.7 4.2 %copy-start.9 = (bf16[128,1024]{1,0:T(8,128)(2,1)S(1)}, bf16[128,1024]{1,0:T(8,128)(2,1)}, u32[]{:S(2)}) copy-start(bf16[128,1024]{1,0:T(8,128)(2,1)} %get-tuple-element.153) | copy-start | bytes 786436 | tf_op jit(solution)/shard_map/cond
  166.7 4.2 %copy-start.12 = (f32[1024,8]{0,1:T(8,128)S(1)}, f32[1024,8]{0,1:T(8,128)}, u32[]{:S(2)}) copy-start(f32[1024,8]{0,1:T(8,128)} %copy-done.11) | copy-start | bytes 98308 | tf_op jit(solution)/shard_map/cond
  166.8 4.2 %copy-start.14 = (f32[1024,8]{0,1:T(8,128)S(1)}, f32[1024,8]{0,1:T(8,128)}, u32[]{:S(2)}) copy-start(f32[1024,8]{0,1:T(8,128)} %copy-done.13) | copy-start | bytes 98308 | tf_op jit(solution)/shard_map/cond
Sparse Core Ops, SparseCore 0:
  10.4 30.8 all-gather.6
  43.8 28.0 all-gather.4
  73.8 27.7 all-gather.8
  109.2 30.4 all-gather.10
where the time goes:
time: 190 us
  blocking collectives  60.7 us (32%)
  waiting for transfers between devices  49.4 us (26%)
  matrix products  22.9 us (12%)
  local copies, waits for them, and re-layouts  22.2 us (12%)
  between operations  16.7 us (9%)
  other arithmetic  14.8 us (8%)
  starting transfers between devices  2.72 us (1%)
    all_gather x1, waiting for transfers between devices, shards(): lax.all_gather(value_rows, 'ctx', axis=0, tiled=True)  26.3 us
    all_gather x1, waiting for transfers between devices, shards(): lax.all_gather(key_rows, 'ctx', axis=0, tiled=True)  23 us
    all_gather x1, blocking collectives, shards(): lax.all_gather(delta_rows, 'ctx', axis=0, tiled=True)  17.9 us
    psum x1, blocking collectives, shards(): grad_filter, grad_gain = lax.psum((tap_terms, gain_terms), 'ctx')  14.2 us
    psum x1, blocking collectives, shards(): square_sum = lax.psum(jnp.sum(attn_wide * attn_wide, axis=1), 'chan')  11.7 us
    unnamed x27, local copies, waits for them, and re-layouts  10.6 us
    all_gather x1, blocking collectives, shards(): lax.all_gather(lse_rows, 'ctx', axis=0, tiled=True)  8.53 us
    psum x1, blocking collectives, shards(): row_dot = lax.psum(jnp.sum(scaled * attn_wide, axis=1), 'chan')  8.37 us
  transfers between devices with their start and end apart: 6, of which 2 were waited for; matrix products, arithmetic and copies ran while one was open for 19% of the time, Pallas kernels for 0%

commit v1 on v0

--- a/solution.py
+++ b/solution.py
@@ -8,6 +8,12 @@
 WIDTH = 4096
 EPS = 1e-06
 NEG = -1e30
+
+
+def add_all(block, mesh_axis):
+    shards = lax.all_gather(block, mesh_axis, axis=0, tiled=False)
+    summed = shards.sum(axis=0)
+    return summed
 
 
 def from_behind(shard, axis, by):
@@ -131,7 +137,7 @@
     )
     lse_rows = lse_sets.T
     attn_wide = outputs.astype(jnp.float32)
-    square_sum = lax.psum(jnp.sum(attn_wide * attn_wide, axis=1), "chan")
+    square_sum = add_all(jnp.sum(attn_wide * attn_wide, axis=1), "chan")
     inverse_rms = 1.0 / jnp.sqrt(square_sum / WIDTH + EPS)
     normed = attn_wide * inverse_rms[:, None] * norm_gain[None, :]
     gate_wide = gate_in.astype(jnp.float32)

time: 190 us -> 190 us (level)
    psum x1 -> x0, blocking collectives: 11.7 us -> none  [shards(): square_sum = lax.psum(jnp.sum(attn_wide * attn_wide, axis=1), 'chan')]
    all_gather x0 -> x1, blocking collectives: none -> 10.9 us  [add_all(): shards = lax.all_gather(block, mesh_axis, axis=0, tiled=False)]
where the time goes in v1:
time: 190 us; the launch traced here: 189 us
  blocking collectives  59.9 us (32%)
  waiting for transfers between devices  49.4 us (26%)
  matrix products  22.9 us (12%)
  local copies, waits for them, and re-layouts  22.2 us (12%)
  between operations  16.7 us (9%)
  other arithmetic  14.9 us (8%)
  starting transfers between devices  2.72 us (1%)
    all_gather x1, waiting for transfers between devices, shards(): lax.all_gather(value_rows, 'ctx', axis=0, tiled=True)  26.3 us
    all_gather x1, waiting for transfers between devices, shards(): lax.all_gather(key_rows, 'ctx', axis=0, tiled=True)  23 us
    all_gather x1, blocking collectives, shards(): lax.all_gather(delta_rows, 'ctx', axis=0, tiled=True)  17.9 us
    psum x1, blocking collectives, shards(): grad_filter, grad_gain = lax.psum((tap_terms, gain_terms), 'ctx')  14.2 us
    all_gather x1, blocking collectives, add_all(): shards = lax.all_gather(block, mesh_axis, axis=0, tiled=False)  10.9 us
    unnamed x27, local copies, waits for them, and re-layouts  10.6 us
    all_gather x1, blocking collectives, shards(): lax.all_gather(lse_rows, 'ctx', axis=0, tiled=True)  8.52 us
    psum x1, blocking collectives, shards(): row_dot = lax.psum(jnp.sum(scaled * attn_wide, axis=1), 'chan')  8.4 us
  transfers between devices with their start and end apart: 6, of which 2 were waited for; matrix products, arithmetic and copies ran while one was open for 19% of the time, Pallas kernels for 0%

profile of v1, /device:TPU:0, one launch (start us, length us, event | category | flops | bytes accessed | tf_op | source)
XLA Modules:
  0.0 188.9 jit_solution(10962953121709948678)
XLA Ops:
  7.2 1.8 copy.102
  9.1 1.8 copy.101
  11.0 1.1 convert_multiply_fusion.1
  12.1 0.8 copy-done.3
  12.9 1.3 collective-permute-start.1
  14.3 0.6 slice.80
  16.8 0.2 copy.103
  17.7 0.2 copy.107
  17.9 0.2 broadcast_in_dim.76
  18.1 0.2 reshape.215
  18.3 23.0 %all-gather.9.cloned.1.call-done = bf16[1024,1024]{0,1:T(8,128)(2,1)} async-done(((bf16[128,1024]{0,1:T(8,128)(2,1)}), bf16[1024,1024]{0,1:T(8,128)(2,1)}) %all-gather.9.cloned.1.call-update) | async-done | bytes 2097168 | tf_op jit(solution)/shard_map/all_gather | solution.py:117
  41.3 3.0 %copy.106 = bf16[1024,8,128]{2,0,1:T(8,128)(2,1)S(1)} copy(bf16[1024,8,128]{0,2,1:T(8,128)(2,1)} %bitcast.152) | data formatting | bytes 4194304
  44.4 1.2 while.35
  44.4 0.1 broadcast_compare_fusion.6
  44.6 0.5 fusion.130
  45.1 0.4 exponential_reduce_fusion.2
  45.6 26.3 %all-gather.7.cloned.1.call-done = bf16[1024,1024]{0,1:T(8,128)(2,1)} async-done(((bf16[128,1024]{0,1:T(8,128)(2,1)}), bf16[1024,1024]{0,1:T(8,128)(2,1)}) %all-gather.7.cloned.1.call-update) | async-done | bytes 2097168 | tf_op jit(solution)/shard_map/all_gather | solution.py:118
  71.9 2.4 %while.36 = (s32[]{:T(128)}, f32[128,8,128]{0,2,1:T(8,128)S(1)}, s32[]{:T(128)}, bf16[1024,8,128]{0,2,1:T(8,128)(2,1)}, bf16[1024,8,128]{2,0,1:T(8,128)(2,1)S(1)...) while((s32[]{:T(128)}, f32[128,8,128]{0,2,1:T(8,128)S(1)}, ...), condition=%wide.region_5.6_spmd.clone, body=%wide.region_4.5_spmd.clone.sunk | while | flops 270729856 | bytes 3549363 | solution.py:72
  72.0 0.1 broadcast_compare_fusion.7
  72.1 2.2 %fusion.134 = f32[128,8,128]{0,2,1:T(8,128)S(1)} fusion(f32[128,8,128]{0,2,1:T(8,128)S(1)} %get-tuple-element.697, bf16[128,8,128]{2,0,1:T(8,128)(2,1)S(1)} %get-tuple-element.713, f32[8,128]{1,0:T(8,128)S(1)} %get-tuple-element.714, bf16[1024,8,128]{2,0,1:T(8,128)(2,1)S(1)} %get-tuple-element.712, s32[]{:T(128)S(6)} %select_n.93, ...), kind=kOutput, calls=%fused_computation.44.clone.1 | convolution fusion | flops 270663680 | bytes 3478528 | tf_op jit(solution)/shard_map/while/body/hrk,khe->rhe/dot_general | solution.py:68
  74.4 1.0 multiply_reduce_fusion.10
  75.3 10.9 %all-gather.1 = f32[4,1,128]{2,1,0:T(1,128)S(1)} all-gather(f32[1,1,128]{2,1,0:T(1,128)S(1)} %bitcast.181), channel_id=2, replica_groups=mesh['ctx'=8,'chan'=4] {'chan'}, dimensions={0}, use_global_device_ids=true | all-gather | bytes 2560 | tf_op jit(solution)/shard_map/all_gather | solution.py:14
  86.2 1.2 copy.124
  87.5 4.0 %multiply_convert_fusion.1 = (bf16[128,1024]{1,0:T(8,128)(2,1)}, f32[128,1024]{1,0:T(8,128)S(1)}) fusion(f32[128,1024]{1,0:T(8,128)S(1)} %copy.124, f32[1024]{0:T(1024)S(1)} %copy-done.10, f32[128]{0:T(128)S(1)} %add_rsqrt_fusion, f32[6,1024]{1,0:T(8,128)S(1)} %collective-permute-done.1, f32[128,1024]{1,0:T(8,128)} %copy-done.3, f32[1024]{0:T(1024)S(1)} %bitcast.163, ...), kind=kLoop, calls=%fused_computation.133 | loop fusion | flops 3014656 | bytes 1892864 | tf_op jit(solution)/shard_map/convert_element_type | solution.py:172
  91.5 0.8 copy-done.1
  92.4 0.2 multiply_reduce_fusion
  92.6 8.4 %psum.21 = f32[128]{0:T(128)S(1)} all-reduce(f32[128]{0:T(128)S(1)} %get-tuple-element.413), channel_id=1, replica_groups=mesh['ctx'=8,'chan'=4] {'chan'}, use_global_device_ids=true, to_apply=%region_9.10 | all-reduce | flops 128 | bytes 1024 | tf_op jit(solution)/shard_map/psum | solution.py:177
  101.0 2.0 %subtract_convert_fusion = (bf16[128,1024]{1,0:T(8,128)(2,1)}, f32[128,1024]{1,0:T(8,128)S(1)}) fusion(f32[128,1024]{1,0:T(8,128)S(1)} %copy.124, f32[128]{0:T(128)S(1)} %fusion.102, f32[1024]{0:T(1024)S(1)} %copy-done.10, f32[128]{0:T(128)S(1)} %add_rsqrt_fusion, f32[128,1024]{1,0:T(8,128)} %copy-done.1, bf16[128,1024]{1,0:T(8,128)(2,1)} %param.19), kind=kLoop, calls=%fused_computation.137 | loop fusion | flops 1310720 | bytes 2102272 | tf_op jit(solution)/shard_map/convert_element_type | solution.py:180
  103.0 0.6 slice.103
  103.7 1.3 collective-permute-start
  104.9 1.0 copy.136
  105.9 0.2 copy.109
  106.2 1.1 multiply_reduce_fusion.8
  107.3 1.0 copy_bitcast_fusion
  108.3 0.9 broadcast.135
  109.2 5.9 %while.37 = (s32[]{:T(128)}, f32[128,8,128]{0,2,1:T(8,128)}, s32[]{:T(128)}, bf16[1024,8,128]{2,0,1:T(8,128)(2,1)S(1)}, bf16[128,8,128]{2,0,1:T(8,128)(2,1)S(1)}...) while((s32[]{:T(128)}, f32[128,8,128]{0,2,1:T(8,128)}, ...), condition=%wide.region_12.13_spmd.clone, body=%wide.region_11.12_spmd.clone.sunk | while | flops 405996160 | bytes 9058503 | solution.py:99
  109.2 1.7 fusion.140
  110.9 0.1 broadcast_compare_fusion.8
  111.1 4.1 %fusion.141 = f32[128,8,128]{0,2,1:T(8,128)} fusion(f32[128,8,128]{0,2,1:T(8,128)} %get-tuple-element.735, f32[8,512,128]{2,1,0:T(8,128)} %fusion.140, bf16[128,8,128]{2,0,1:T(8,128)(2,1)S(1)} %get-tuple-element.755, f32[8,128]{1,0:T(8,128)S(1)} %get-tuple-element.756, bf16[1024,8,128]{0,2,1:T(8,128)(2,1)} %get-tuple-element.754, s32[]{:T(128)S(6)} %select_n.95, ...), kind=kOutput, calls=%fused_computation.64.clone.1 | convolution fusion | flops 271712256 | bytes 5579776 | tf_op jit(solution)/shard_map/while/body/hrk,khe->rhe/dot_general | solution.py:95
  115.2 1.1 multiply_convert_fusion.3
  116.3 0.8 copy.125
  117.1 17.9 %all_gather.31 = f32[1024,8]{0,1:T(8,128)S(1)} all-gather(f32[128,8]{0,1:T(8,128)S(1)} %bitcast.179), channel_id=1, replica_groups=mesh['ctx'=8,'chan'=4] {'ctx'}, dimensions={0}, use_global_device_ids=true | all-gather | bytes 36864 | tf_op jit(solution)/shard_map/all_gather | solution.py:199
  135.0 8.5 %all_gather.29 = f32[1024,8]{0,1:T(8,128)S(1)} all-gather(f32[128,8]{0,1:T(8,128)S(1)} %bitcast.180), channel_id=1, replica_groups=mesh['ctx'=8,'chan'=4] {'ctx'}, dimensions={0}, use_global_device_ids=true | all-gather | bytes 36864 | tf_op jit(solution)/shard_map/all_gather | solution.py:198
  143.6 1.2 fusion.78
  144.8 1.2 multiply_reduce_fusion.1
  146.1 0.1 reshape.221
  146.2 0.1 reshape.222
  146.6 0.1 reduce_sum.185
  146.7 0.1 reduce_sum.187
  146.9 0.1 reduce_sum.189
  147.0 0.1 reduce_sum.191
  147.1 0.1 reduce_sum.193
  147.2 0.1 reduce_sum.195
  147.3 0.1 reduce_sum.197
  147.5 14.2 %all-reduce = (f32[128,7]{0,1:T(8,128)}, f32[1024]{0:T(1024)}) all-reduce(f32[128,7]{0,1:T(8,128)S(1)} %stack.31, f32[1024]{0:T(1024)S(1)} %get-tuple-element.412), channel_id=1, replica_groups=mesh['ctx'=8,'chan'=4] {'ctx'}, use_global_device_ids=true, to_apply=%region_29.30 | all-reduce | flops 1920 | bytes 15360 | tf_op jit(solution)/shard_map/psum | solution.py:175
  161.7 19.8 %conditional.1 = (f32[128,8,128]{0,2,1:T(8,128)S(1)}, bf16[128,1024]{1,0:T(8,128)(2,1)}) conditional(s32[]{:T(128)} %convert_element_type.91, () %tuple.33, (s32[128]{0:T(128)S(1)}, bf16[1024,1024]{1,0:T(8,128)(2,1)}, bf16[128,1024]{1,0:T(8,128)(2,1)S(1)}, f32[1024,8]{0,1:T(8,128)S(1)}, bf16[1024,1024]{1,0:T(8,128)(2,1)}, ...), branch_computations={%region_13.14_spmd, %region_14.15_spmd} | conditional | flops 1084489728 | bytes 38503096 | solution.py:235
  161.7 4.3 %fusion.11 = f32[8,1024,128]{2,1,0:T(8,128)} fusion(bf16[1024,1024]{1,0:T(8,128)(2,1)} %get-tuple-element.149, bf16[128,1024]{1,0:T(8,128)(2,1)S(1)} %get-tuple-element.150), kind=kOutput, calls=%fused_computation.9 | convolution fusion | flops 268435456 | bytes 6553600 | tf_op jit(solution)/shard_map/cond/branch_1_fun/rhe,khe->hrk/dot_general | solution.py:26
  166.0 4.1 %copy.115 = bf16[1024,1024]{0,1:T(8,128)(2,1)} copy(bf16[1024,1024]{1,0:T(8,128)(2,1)} %get-tuple-element.399) | data formatting | bytes 4194304 | tf_op jit(solution)/shard_map
  170.1 0.1 iota_compare_fusion
  170.2 6.4 %fusion.19 = f32[128,8,128]{2,0,1:T(8,128)S(1)} fusion(f32[8,1024,128]{2,1,0:T(8,128)} %fusion.11, bf16[1024,8,128]{0,2,1:T(8,128)(2,1)} %bitcast.153, f32[8,1024]{1,0:T(8,128)S(1)} %bitcast.175, f32[8,1024]{1,0:T(8,128)S(1)} %bitcast.177, pred[1024,128]{1,0:T(8,128)(4,1)S(1)} %iota_compare_fusion, bf16[1024,1024]{1,0:T(8,128)(2,1)S(1)} %copy-done.4, ...), kind=kOutput, calls=%fused_computation.17 | convolution fusion | flops 543162368 | bytes 9371648 | tf_op jit(solution)/shard_map/cond/branch_1_fun/hrk,rhe->khe/dot_general | solution.py:221
  176.6 0.2 copy.128
  176.9 3.8 %fusion.22 = bf16[8,128,128]{1,2,0:T(8,128)(2,1)S(1)} fusion(bf16[1024,8,128]{0,2,1:T(8,128)(2,1)} %bitcast.154, f32[8,1024,128]{2,1,0:T(8,128)} %fusion.11, f32[8,1024]{1,0:T(8,128)} %bitcast.176, pred[1024,128]{1,0:T(8,128)(4,1)S(1)} %iota_compare_fusion), kind=kOutput, calls=%fused_computation.18 | convolution fusion | flops 272760832 | bytes 6717440 | tf_op jit(solution)/shard_map/cond/branch_1_fun/hrk,rhe->khe/dot_general | solution.py:224
  180.6 0.8 copy.130
  181.6 0.8 copy.126
  (68 shorter events, 1.0 us)
Async XLA Ops:
  7.2 9.7 %copy-start.6 = (bf16[128,1024]{1,0:T(8,128)(2,1)S(1)}, bf16[128,1024]{1,0:T(8,128)(2,1)}, u32[]{:S(2)}) copy-start(bf16[128,1024]{1,0:T(8,128)(2,1)} %param.16) | copy-start | bytes 786436
  7.2 10.7 %copy-start.15 = (f32[128,7]{0,1:T(8,128)S(1)}, f32[128,7]{0,1:T(8,128)}, u32[]{:S(2)}) copy-start(f32[128,7]{0,1:T(8,128)} %param.21) | copy-start | bytes 10756
  7.2 34.1 %all-gather.9.cloned.1.call-start = ((), (), s32[]{:S(2)}) async-start(), calls=%async_computation.1 | async-start | bytes 2359296 | tf_op jit(solution)/shard_map/all_gather | solution.py:117
  9.1 62.8 %all-gather.7.cloned.1.call-start = ((), (), s32[]{:S(2)}) async-start(), calls=%async_computation | async-start | bytes 2359296 | tf_op jit(solution)/shard_map/all_gather | solution.py:118
  10.9 150.7 %all-gather.11.cloned.1.call-start = ((), (), s32[]{:S(2)}) async-start(), calls=%async_computation.2 | async-start | bytes 2359296 | tf_op jit(solution)/shard_map/all_gather | solution.py:205
  12.1 0.8 copy-start.3
  12.9 74.6 %collective-permute-start.1 = (f32[6,1024]{1,0:T(8,128)S(1)}, f32[6,1024]{1,0:T(8,128)S(1)}, u32[]{:S(2)}, u32[]{:S(2)}) collective-permute-start(f32[6,1024]{1,0:T(8,128)S(1)} %slice.119), channel_id=1, source_target_pairs={{4,0},{8,4},{12,8},{16,12},{20,16},{24,20},{28,24},{5,1},{9,5},{13... | collective-permute-start | bytes 73736 | tf_op jit(solution)/shard_map/ppermute | solution.py:22
  14.2 147.5 %all-gather.13.cloned.1.call-start = ((), (), s32[]{:S(2)}) async-start(), calls=%async_computation.3 | async-start | bytes 2359296 | tf_op jit(solution)/shard_map/all_gather | solution.py:206
  74.3 18.2 %copy-start = (f32[128,8,128]{0,2,1:T(8,128)}, f32[128,8,128]{0,2,1:T(8,128)S(1)}, u32[]{:S(2)}) copy-start(f32[128,8,128]{0,2,1:T(8,128)S(1)} %get-tuple-element.171) | copy-start | bytes 1572868
  74.4 13.2 %copy-start.10 = (f32[1024]{0:T(1024)S(1)}, f32[1024]{0:T(1024)}, u32[]{:S(2)}) copy-start(f32[1024]{0:T(1024)} %param.22) | copy-start | bytes 12292
  87.5 4.9 %copy-start.7 = (bf16[128,1024]{1,0:T(8,128)(2,1)S(1)}, bf16[128,1024]{1,0:T(8,128)(2,1)}, u32[]{:S(2)}) copy-start(bf16[128,1024]{1,0:T(8,128)(2,1)} %param.19) | copy-start | bytes 786436
  91.5 0.8 copy-start.1
  103.7 39.9 %collective-permute-start = (f32[6,1024]{1,0:T(8,128)}, f32[6,1024]{1,0:T(8,128)S(1)}, u32[]{:S(2)}, u32[]{:S(2)}) collective-permute-start(f32[6,1024]{1,0:T(8,128)} %slice.103), channel_id=1, source_target_pairs={{0,4},{4,8},{8,12},{12,16},{16,20},{20,24},{24,28},{1,5},{5,9},{9,... | collective-permute-start | bytes 73736 | tf_op jit(solution)/shard_map/ppermute | solution.py:22
  109.2 34.4 %copy-start.2 = (bf16[128,1024]{1,0:T(8,128)(2,1)S(1)}, bf16[128,1024]{1,0:T(8,128)(2,1)}, u32[]{:S(2)}) copy-start(bf16[128,1024]{1,0:T(8,128)(2,1)} %param.23) | copy-start | bytes 786436
  115.2 29.6 %copy-start.8 = (bf16[128,1024]{1,0:T(8,128)(2,1)S(1)}, bf16[128,1024]{1,0:T(8,128)(2,1)}, u32[]{:S(2)}) copy-start(bf16[128,1024]{1,0:T(8,128)(2,1)} %param.20) | copy-start | bytes 786436
  143.6 18.1 %copy-start.5 = (bf16[128,1024]{1,0:T(8,128)(2,1)S(1)}, bf16[128,1024]{1,0:T(8,128)(2,1)}, u32[]{:S(2)}) copy-start(bf16[128,1024]{1,0:T(8,128)(2,1)} %param.17) | copy-start | bytes 786436
  161.7 4.3 %copy-start.11 = (f32[1024,8]{0,1:T(8,128)}, f32[1024,8]{0,1:T(8,128)S(1)}, u32[]{:S(2)}) copy-start(f32[1024,8]{0,1:T(8,128)S(1)} %get-tuple-element.154) | copy-start | bytes 98308 | tf_op jit(solution)/shard_map/cond
  161.7 4.3 %copy-start.13 = (f32[1024,8]{0,1:T(8,128)}, f32[1024,8]{0,1:T(8,128)S(1)}, u32[]{:S(2)}) copy-start(f32[1024,8]{0,1:T(8,128)S(1)} %get-tuple-element.151) | copy-start | bytes 98308 | tf_op jit(solution)/shard_map/cond
  166.0 4.2 %copy-start.4 = (bf16[1024,1024]{1,0:T(8,128)(2,1)S(1)}, bf16[1024,1024]{1,0:T(8,128)(2,1)}, u32[]{:S(2)}) copy-start(bf16[1024,1024]{1,0:T(8,128)(2,1)} %get-tuple-element.149) | copy-start | bytes 6291460 | tf_op jit(solution)/shard_map/cond
  166.0 4.2 %copy-start.9 = (bf16[128,1024]{1,0:T(8,128)(2,1)S(1)}, bf16[128,1024]{1,0:T(8,128)(2,1)}, u32[]{:S(2)}) copy-start(bf16[128,1024]{1,0:T(8,128)(2,1)} %get-tuple-element.153) | copy-start | bytes 786436 | tf_op jit(solution)/shard_map/cond
  166.0 4.2 %copy-start.12 = (f32[1024,8]{0,1:T(8,128)S(1)}, f32[1024,8]{0,1:T(8,128)}, u32[]{:S(2)}) copy-start(f32[1024,8]{0,1:T(8,128)} %copy-done.11) | copy-start | bytes 98308 | tf_op jit(solution)/shard_map/cond
  166.0 4.2 %copy-start.14 = (f32[1024,8]{0,1:T(8,128)S(1)}, f32[1024,8]{0,1:T(8,128)}, u32[]{:S(2)}) copy-start(f32[1024,8]{0,1:T(8,128)} %copy-done.13) | copy-start | bytes 98308 | tf_op jit(solution)/shard_map/cond
Sparse Core Ops, SparseCore 0:
  10.4 30.8 all-gather.8
  43.8 28.0 all-gather.6
  73.8 27.7 all-gather.10
  108.4 30.4 all-gather.12
